TPU v7x, 128 devices: a whole 4x4x4 slice. The times are simulated.
128 devices in a mesh: req: 16 (over z, y), tp: 8 (over x, core).
Axes of the slice: x: 4, y: 4, z: 4, core: 2. Of those that a mesh axis runs over, the one named last changes fastest.
Arguments:
- hidden_in: bfloat16 [4096, 1024], P('req'), may hold values from -42 to 42
- prompt_kv: bfloat16 [2, 128, 512, 1024], P(None, 'req', None, 'tp'), may hold values from -9 to 9
- tail_kv: bfloat16 [2, 4096, 64, 1024], P(None, 'req', None, 'tp'), may hold values from -9 to 9
- group_of: int32 [4096], P('req'), may hold values from 0 to 7
- prompt_len: int32 [128], P('req'), may hold values from 64 to 512, as said below
- tail_len: int32 [4096], P('req'), may hold values from 0 to 63, as said below
- bucket_of: int32 [577], replicated, may hold values from 0 to 31, never falling along the last dimension, each value on 1 to 38 neighbouring positions
- bias_table: float32 [32, 16], P(None, 'tp'), may hold values from -6 to 302
- attn_gain: float32 [1024], replicated, may hold values from 0.1 to 1.9
- w_query: bfloat16 [1024, 1024], P(None, 'tp'), may hold values from -0.1875 to 0.1875
- w_key: bfloat16 [1024, 1024], P(None, 'tp'), may hold values from -0.1875 to 0.1875
- w_value: bfloat16 [1024, 1024], P(None, 'tp'), may hold values from -0.1875 to 0.1875
- w_out: bfloat16 [1024, 1024], P('tp'), may hold values from -0.75 to 0.75
- ffn_gain: float32 [1024], replicated, may hold values from 0.1 to 1.9
- router_weight: bfloat16 [1024, 16], replicated, may hold values from -0.1875 to 0.1875
- expert_ids: int32 [4096, 2], P('req'), may hold values from 0 to 15, all different within a row; in each aligned block of 256 rows (0 to 255, 256 to 511, ...) at most 40 rows name the same one
- w_gate: bfloat16 [16, 1024, 2816], P('req', None, 'tp'), may hold values from -0.1875 to 0.1875
- w_up: bfloat16 [16, 1024, 2816], P('req', None, 'tp'), may hold values from -0.1875 to 0.1875
- w_down: bfloat16 [16, 2816, 1024], P('req', 'tp'), may hold values from -0.109375 to 0.109375
- new_slot: int32 [4096], replicated, may hold values from 0 to 4095, as said below
Outputs:
- out_hidden: bfloat16 [4096, 1024], P('req')
- new_tail_kv: bfloat16 [2, 4096, 64, 1024], P(None, 'req', None, 'tp')
Inputs may be any that keep to these rules, and one draw needn't show every extreme that they name: `expert_ids`: in each replica's aligned block of 256 tokens no expert is named by more than 40 of them, a bound that some block reaches. `new_slot`: A permutation. Exactly 4 requests of each replica are movers; all movers of one replica go to one replica (possibly itself), each taking a slot that a mover of that replica leaves; every other request keeps its slot. `prompt_len`: each replica has a group of 512 rows. `tail_len`: each replica has a request of 63 own rows and one of none.
All inputs are finite; a program needn't handle non-finite values.
Results may differ from a plain program's by a relative error of at most 0.013.
Values may be sent and summed in bfloat16 or wider, within the bound.
A program may use at most 128 MiB of HBM per device.

v0:
```python
import jax
import jax.numpy as jnp
from jax import lax
from jax.sharding import PartitionSpec as P

HD = 64
TOP = 2
MIG = 4
EPS = 1e-06


def rms_scale(values, gain):
    v = values.astype(jnp.float32)
    return (v * lax.rsqrt(jnp.mean(v * v, axis=-1, keepdims=True) + EPS) * gain).astype(
        jnp.bfloat16
    )


def bias_lookup(distance, starts, finish, bias_table):
    within = (distance[..., None] >= starts) & (distance[..., None] < finish)
    return jnp.einsum(
        "rjk,kh->hrj", within.astype(jnp.float32), bias_table, precision=lax.Precision.HIGHEST
    )


def attention(
    hidden_in,
    prompt_kv,
    tail_kv,
    group_of,
    prompt_len,
    tail_len,
    bucket_of,
    bias_table,
    attn_gain,
    w_query,
    w_key,
    w_value,
):
    normed = rms_scale(hidden_in, attn_gain)
    query = jnp.dot(normed, w_query, preferred_element_type=jnp.float32).astype(jnp.bfloat16)
    key_new = jnp.dot(normed, w_key, preferred_element_type=jnp.float32).astype(jnp.bfloat16)
    value_new = jnp.dot(normed, w_value, preferred_element_type=jnp.float32).astype(jnp.bfloat16)
    rows = hidden_in.shape[0]
    heads_here = w_query.shape[1] // HD
    groups_here = prompt_kv.shape[1]
    prompt_rows = prompt_kv.shape[2]
    tail_rows = tail_kv.shape[2]
    span = bucket_of.shape[0]
    buckets = bias_table.shape[0]
    bucket_ids = jnp.arange(buckets, dtype=jnp.int32)
    starts = jnp.sum((bucket_of[:, None] < bucket_ids[None, :]).astype(jnp.int32), axis=0)
    finish = jnp.concatenate([starts[1:], jnp.full((1,), span, jnp.int32)])
    first_bias = jnp.sum(jnp.where((bucket_ids == bucket_of[0])[:, None], bias_table, 0.0), axis=0)
    scale = HD ** (-0.5)
    q = query.reshape(rows, heads_here, HD)
    pk = prompt_kv[0].reshape(groups_here, prompt_rows, heads_here, HD)
    pv = prompt_kv[1].reshape(groups_here, prompt_rows, heads_here, HD)
    tk = tail_kv[0].reshape(rows, tail_rows, heads_here, HD)
    tv = tail_kv[1].reshape(rows, tail_rows, heads_here, HD)
    kn = key_new.reshape(rows, heads_here, HD)
    vn = value_new.reshape(rows, heads_here, HD)
    group_hit = group_of[:, None] == jnp.arange(groups_here, dtype=jnp.int32)[None, :]
    own_len = jnp.sum(jnp.where(group_hit, prompt_len[None, :], 0), axis=1)
    pos = own_len + tail_len
    jpos = jnp.arange(prompt_rows, dtype=jnp.int32)
    pidx = jnp.clip(pos[:, None] - jpos[None, :], 0, span - 1)
    pbias = bias_lookup(pidx, starts, finish, bias_table)
    pmask = group_hit[:, :, None] & (jpos[None, None, :] < own_len[:, None, None])
    ps = (
        jnp.einsum("rhd,gjhd->hrgj", q, pk, preferred_element_type=jnp.float32) * scale
        + pbias[:, :, None, :]
    )
    ps = jnp.where(pmask[None], ps, -jnp.inf)
    tpos = jnp.arange(tail_rows, dtype=jnp.int32)
    tidx = jnp.clip(tail_len[:, None] - tpos[None, :], 0, span - 1)
    tbias = bias_lookup(tidx, starts, finish, bias_table)
    tmask = tpos[None, :] < tail_len[:, None]
    ts = jnp.einsum("rhd,rthd->hrt", q, tk, preferred_element_type=jnp.float32) * scale + tbias
    ts = jnp.where(tmask[None], ts, -jnp.inf)
    ns = (
        jnp.einsum("rhd,rhd->hr", q, kn, preferred_element_type=jnp.float32) * scale
        + first_bias[:, None]
    )
    top = jnp.maximum(jnp.maximum(jnp.max(ps, axis=(2, 3)), jnp.max(ts, axis=2)), ns)
    pe = jnp.exp(ps - top[:, :, None, None])
    te = jnp.exp(ts - top[:, :, None])
    ne = jnp.exp(ns - top)
    total = jnp.sum(pe, axis=(2, 3)) + jnp.sum(te, axis=2) + ne
    pw = (pe / total[:, :, None, None]).astype(jnp.bfloat16)
    tw = (te / total[:, :, None]).astype(jnp.bfloat16)
    nw = (ne / total).astype(jnp.bfloat16)
    head = jnp.einsum("hrgj,gjhd->rhd", pw, pv, preferred_element_type=jnp.float32)
    head = head + jnp.einsum("hrt,rthd->rhd", tw, tv, preferred_element_type=jnp.float32)
    head = head + jnp.einsum("hr,rhd->rhd", nw, vn, preferred_element_type=jnp.float32)
    head_out = head.reshape(rows, heads_here * HD).astype(jnp.bfloat16)
    return (head_out, key_new, value_new, tmask)


def body(
    hidden_in,
    prompt_kv,
    tail_kv,
    group_of,
    prompt_len,
    tail_len,
    bucket_of,
    bias_table,
    attn_gain,
    w_query,
    w_key,
    w_value,
    w_out,
    ffn_gain,
    router_weight,
    expert_ids,
    w_gate,
    w_up,
    w_down,
    new_slot,
):
    head_out, key_new, value_new, tmask = attention(
        hidden_in,
        prompt_kv,
        tail_kv,
        group_of,
        prompt_len,
        tail_len,
        bucket_of,
        bias_table,
        attn_gain,
        w_query,
        w_key,
        w_value,
    )
    rows = hidden_in.shape[0]
    width = hidden_in.shape[1]
    local_idx = jnp.arange(rows, dtype=jnp.int32)
    tail_rows = tail_kv.shape[2]
    write_row = jnp.arange(tail_rows, dtype=jnp.int32)[None, :] == tail_len[:, None]
    fresh = jnp.stack([key_new, value_new])[:, :, None, :]
    tail_new = jnp.where(write_row[None, :, :, None], fresh, tail_kv)
    partial_attn = jnp.dot(head_out, w_out, preferred_element_type=jnp.float32)
    attn = lax.psum(partial_attn, "tp")
    resid = (hidden_in.astype(jnp.float32) + attn).astype(jnp.bfloat16)
    normed2 = rms_scale(resid, ffn_gain)
    logits = jnp.dot(normed2, router_weight, preferred_element_type=jnp.float32)
    experts = router_weight.shape[1]
    expert_range = jnp.arange(experts, dtype=jnp.int32)
    first_hit = expert_ids[:, 0:1] == expert_range[None, :]
    second_hit = expert_ids[:, 1:2] == expert_range[None, :]
    picked_first = jnp.sum(jnp.where(first_hit, logits, 0.0), axis=1)
    picked_second = jnp.sum(jnp.where(second_hit, logits, 0.0), axis=1)
    gate_first = jax.nn.sigmoid(picked_first - picked_second)
    capacity = 5 * rows * TOP // (4 * experts)
    flat_e = expert_ids.reshape(-1)
    onehot = (flat_e[:, None] == expert_range[None, :]).astype(jnp.int32)
    slot_pos = jnp.sum((jnp.cumsum(onehot, axis=0) - 1) * onehot, axis=1)
    target = flat_e * capacity + slot_pos
    placed = (target[:, None] == jnp.arange(experts * capacity, dtype=jnp.int32)[None, :]).astype(
        jnp.bfloat16
    )
    doubled = jnp.repeat(normed2, TOP, axis=0)
    outgoing = (
        jnp.dot(placed.T, doubled, preferred_element_type=jnp.float32)
        .astype(jnp.bfloat16)
        .reshape(experts, capacity, width)
    )
    gate_mat = w_gate[0]
    up_mat = w_up[0]
    down_mat = w_down[0]
    received = lax.all_to_all(outgoing, "req", split_axis=0, concat_axis=0, tiled=True)
    flat = received.reshape(-1, received.shape[-1])
    gate_h = jnp.dot(flat, gate_mat, preferred_element_type=jnp.float32)
    up_h = jnp.dot(flat, up_mat, preferred_element_type=jnp.float32)
    act = (jax.nn.gelu(gate_h, approximate=True) * up_h).astype(jnp.bfloat16)
    summed = lax.psum(
        jnp.dot(act, down_mat, preferred_element_type=jnp.float32).astype(jnp.bfloat16), "tp"
    )
    back = summed.reshape(received.shape)
    result = lax.all_to_all(back, "req", split_axis=0, concat_axis=0, tiled=True)
    pair_out = jnp.dot(
        placed, result.reshape(experts * capacity, width), preferred_element_type=jnp.float32
    ).reshape(rows, TOP, width)
    mixed = (
        resid.astype(jnp.float32)
        + gate_first[:, None] * pair_out[:, 0]
        + (1.0 - gate_first)[:, None] * pair_out[:, 1]
    ).astype(jnp.bfloat16)
    replicas = lax.axis_size("req")
    me = lax.axis_index("req")
    total_reqs = new_slot.shape[0]
    everyone = jnp.arange(total_reqs, dtype=jnp.int32)
    leaving_all = new_slot // rows != everyone // rows
    rank_all = (
        jnp.cumsum(leaving_all.reshape(replicas, rows).astype(jnp.int32), axis=1) - 1
    ).reshape(-1)
    source_of = jnp.zeros((total_reqs,), jnp.int32).at[new_slot].set(everyone)
    first_slot = me * rows
    leaving = lax.dynamic_slice_in_dim(leaving_all, first_slot, rows, 0)
    my_rank = lax.dynamic_slice_in_dim(rank_all, first_slot, rows, 0)
    send_idx = (
        jnp.zeros((MIG,), jnp.int32)
        .at[jnp.where(leaving, my_rank, MIG)]
        .set(local_idx, mode="drop")
    )
    send_rows = mixed[send_idx]
    send_tail = jnp.swapaxes(tail_new[:, send_idx], 0, 1)
    got_rows, got_tail = (
        lax.all_gather(send_rows, "req", axis=0, tiled=True),
        lax.all_gather(send_tail, "req", axis=0, tiled=True),
    )
    count = jnp.sum(leaving.astype(jnp.int32))
    vacated = jnp.where(jnp.arange(MIG, dtype=jnp.int32) < count, send_idx, rows)
    source = source_of[first_slot + jnp.minimum(vacated, rows - 1)]
    position = source // rows * MIG + rank_all[source]
    position = jnp.clip(position, 0, got_rows.shape[0] - 1)
    out_hidden = mixed.at[vacated].set(got_rows[position], mode="drop")
    new_tail_kv = tail_new.at[:, vacated].set(jnp.swapaxes(got_tail[position], 0, 1), mode="drop")
    return (out_hidden, new_tail_kv)


def solution(mesh):
    return jax.shard_map(
        body,
        mesh=mesh,
        in_specs=(
            P("req", None),
            P(None, "req", None, "tp"),
            P(None, "req", None, "tp"),
            P("req"),
            P("req"),
            P("req"),
            P(),
            P(None, "tp"),
            P(),
            P(None, "tp"),
            P(None, "tp"),
            P(None, "tp"),
            P("tp", None),
            P(),
            P(),
            P("req", None),
            P("req", None, "tp"),
            P("req", None, "tp"),
            P("req", "tp", None),
            P(),
        ),
        out_specs=(P("req", None), P(None, "req", None, "tp")),
        check_vma=False,
    )
```

profile of v0, /device:TPU:6, one launch (start us, length us, event | category | flops | bytes accessed | tf_op | source)
XLA Modules:
  0.0 309.5 jit_solution(10653071250375701447)
XLA Ops:
  8.1 1.3 iota_compare_fusion.11
  9.3 0.8 select_reduce_fusion.2
  10.3 0.7 add.171
  10.9 1.3 iota_compare_fusion.5
  12.2 1.3 subtract_clamp_fusion.1
  13.6 0.8 convert_reduce_fusion
  14.4 1.2 slice.45
  15.9 6.9 %fusion.8 = f32[2,256,512]{2,0,1:T(2,128)S(1)} fusion(s32[256,512]{1,0:T(8,128)S(1)} %subtract_clamp_fusion, s32[32]{0:T(128)S(1)} %pad_add_fusion, s32[32]{0:T(128)S(1)} %convert_reduce_fusion, f32[32,2]{0,1:T(2,128)} %param.27), kind=kOutput, calls=%fused_computation.35 | convolution fusion | flops 113246208 | bytes 1573376 | tf_op jit(solution)/shard_map/rjk,kh->hrj/dot_general | solution.py:21
  22.8 0.2 copy.78
  23.0 0.2 fusion.20
  23.2 1.2 fusion.90
  24.5 1.3 copy.113
  25.8 6.5 %fusion.89 = (bf16[1,256,64,128]{3,2,1,0:T(8,128)(2,1)}, bf16[1,256,64,128]{3,2,1,0:T(8,128)(2,1)}) fusion(bf16[2,256,64,128]{3,2,1,0:T(8,128)(2,1)} %param.22), kind=kLoop, calls=%fused_computation.187 | loop fusion | bytes 16777216 | tf_op jit(solution)/shard_map/slice | solution.py:59
  32.3 7.0 %copy.114 = bf16[1,256,64,128]{1,3,2,0:T(8,128)(2,1)} copy(bf16[1,256,64,128]{3,2,1,0:T(8,128)(2,1)} %get-tuple-element.12) | data formatting | bytes 8388608
  39.4 0.4 bitcast_convert_fusion.1
  39.8 1.1 convolution_convert_fusion.3
  40.8 0.7 iota_compare_fusion.12
  41.6 1.3 broadcast_and_fusion
  42.9 3.7 %multiply_reduce_fusion.1 = f32[2,256,64]{1,0,2:T(2,128)S(1)} fusion(bf16[2,256,64,64]{1,2,0,3:T(8,128)(2,1)} %bitcast.145, f32[2,256,64]{1,2,0:T(8,128)S(1)} %get-tuple-element.27), kind=kLoop, calls=%fused_computation.13 | loop fusion | flops 6258688 | bytes 4456448 | tf_op jit(solution)/shard_map/rhd,rthd->hrt/dot_general | solution.py:79
  46.7 0.9 fusion.92
  47.6 2.2 fusion.5
  49.9 2.7 fusion.4
  52.7 0.6 copy-done.1
  53.4 0.7 convert_bitcast_fusion
  54.2 0.5 copy-done.17
  54.7 6.9 %copy.116 = bf16[1,256,64,128]{1,3,2,0:T(8,128)(2,1)} copy(bf16[1,256,64,128]{3,2,1,0:T(8,128)(2,1)} %get-tuple-element.13) | data formatting | bytes 8388608
  61.6 2.0 convolution_convert_fusion.2
  63.6 2.3 copy.115
  65.9 3.2 %multiply_reduce_fusion = f32[256,2,64]{0,2,1:T(8,128)S(1)} fusion(bf16[256,2,64,64]{0,3,1,2:T(8,128)(2,1)} %bitcast.146, f32[256,2,64]{0,1,2:T(2,128)S(1)} %bitcast_convert_fusion), kind=kLoop, calls=%fused_computation.12 | loop fusion | flops 6258688 | bytes 4456448 | tf_op jit(solution)/shard_map/hrt,rthd->rhd/dot_general | solution.py:94
  69.2 5.1 %fusion.19 = bf16[256,2,64]{0,2,1:T(8,128)(2,1)S(1)} fusion(f32[256,2,64]{0,2,1:T(8,128)S(1)} %multiply_reduce_fusion, f32[2,256,8,512]{3,1,2,0:T(8,128)} %copy-done.1, f32[2,256]{1,0:T(2,128)S(1)} %copy-done.18, f32[2,256]{1,0:T(2,128)S(1)} %copy-done.13, f32[2,256,512]{2,1,0:T(8,128)S(1)} %copy.78, pred[256,8,512]{2,0,1:T(8,128)(4,1)S(1)} %broadcast_and_fusion, ...), kind=kOutput, calls=%fused_computation.52 | convolution fusion | flops 281182208 | bytes 11802624 | tf_op jit(solution)/shard_map/hrgj,gjhd->rhd/dot_general | solution.py:93
  74.3 1.3 fusion.93
  76.1 1.2 reduce-window.14
  77.2 0.2 slice_reduce_fusion
  77.6 60.5 %all-reduce.3.cloned.1.call-done = f32[256,1024]{1,0:T(8,128)} async-done(((f32[256,1024]{1,0:T(8,128)}), f32[256,1024]{1,0:T(8,128)}) %all-reduce.3.cloned.1.call-update) | async-done | bytes 1048592 | tf_op jit(solution)/shard_map/psum | solution.py:144
  138.1 1.5 fusion.24
  139.6 0.2 fusion.26
  139.8 0.5 broadcast_in_dim.97
  140.4 1.2 reshape.353
  141.6 3.2 %convolution_convert_fusion.1 = bf16[640,1024]{1,0:T(8,128)(2,1)} fusion(bf16[512,1024]{1,0:T(8,128)(2,1)} %reshape.353, s32[512]{0:T(512)S(1)} %multiply_add_fusion), kind=kOutput, calls=%fused_computation.28 | convolution fusion | flops 672071680 | bytes 2361344 | tf_op jit(solution)/shard_map/dot_general | solution.py:165
  144.9 7.0 %all-to-all-start = ((bf16[16,40,1024]{2,1,0:T(8,128)(2,1)}), bf16[16,40,1024]{2,1,0:T(8,128)(2,1)S(1)}, u32[]{:S(2)}, u32[]{:S(2)}) async-start(bf16[16,40,1024]{2,1,0:T(8,128)(2,1)} %bitcast.149), calls=%async_computation | async-start | bytes 2621440 | tf_op jit(solution)/shard_map/all_to_all | solution.py:172
  152.0 0.6 reduce-window.16
  152.6 0.2 slice_reduce_fusion.1
  153.2 0.7 convert_reduce_fusion.1
  153.9 1.4 scatter_custom_fusion
  155.3 0.7 compare_select_fusion.2
  156.0 20.2 %all-to-all-done = bf16[16,40,1024]{2,1,0:T(8,128)(2,1)S(1)} async-done(((bf16[16,40,1024]{2,1,0:T(8,128)(2,1)}), bf16[16,40,1024]{2,1,0:T(8,128)(2,1)S(1)}, u32[]{:S(2)}, u32[]{:S(2)}) %all-to-all-start) | async-done | bytes 1310752 | tf_op jit(solution)/shard_map/all_to_all | solution.py:172
  176.1 2.8 fusion.48
  178.9 4.3 %convolution_convert_fusion = bf16[640,1024]{1,0:T(8,128)(2,1)} fusion(bf16[640,1024]{1,0:T(8,128)(2,1)S(1)} %bitcast.148, f32[640,352]{0,1:T(8,128)} %fusion.48, bf16[1,352,1024]{2,1,0:T(8,128)(2,1)S(1)} %copy-done, bf16[1,1024,352]{1,2,0:T(8,128)(2,1)} %param.37), kind=kOutput, calls=%fused_computation.27 | convolution fusion | flops 925655040 | bytes 4964352 | tf_op jit(solution)/shard_map/dot_general | solution.py:178
  183.3 8.3 %broadcast_select_fusion = bf16[2,256,64,128]{3,2,1,0:T(8,128)(2,1)} fusion(bf16[2,256,64,128]{3,2,1,0:T(8,128)(2,1)} %param.22, pred[256,64]{1,0:T(8,128)(4,1)S(1)} %copy.89, bf16[2,256,128]{2,1,0:T(8,128)(2,1)S(1)} %copy.90), kind=kLoop, calls=%fused_computation.20 | loop fusion | flops 4194304 | bytes 16924672 | tf_op jit(solution)/shard_map/jit(_where)/select_n | solution.py:142
  191.5 4.7 %gather_fusion.3 = bf16[4,2,64,128]{3,2,1,0:T(8,128)(2,1)} fusion(bf16[2,256,64,128]{3,2,1,0:T(8,128)(2,1)} %broadcast_select_fusion, s32[1024]{0:T(1024)S(1)} %pad_clamp_fusion.3), kind=kCustom, calls=%fused_computation.4 | custom fusion | bytes 262160 | tf_op jit(solution)/shard_map/gather | solution.py:208
  196.5 15.5 %scatter_custom_fusion.1 = s32[4096]{0:T(1024)S(1)} fusion(s32[4096]{0:T(1024)S(1)} %add_select_fusion.1, s32[4096]{0:T(1024)S(1)} %iota.80, s32[]{:T(128)} %constant.36.clone.1), kind=kCustom, calls=%fused_computation.136 | custom fusion | bytes 16388 | tf_op jit(solution)/shard_map/scatter | solution.py:198
  212.0 0.6 gather_fusion.1
  212.7 28.9 %all-reduce.5.cloned.1.call-done = bf16[16,40,1024]{2,1,0:T(8,128)(2,1)} async-done(((bf16[16,40,1024]{2,1,0:T(8,128)(2,1)}), bf16[16,40,1024]{2,1,0:T(8,128)(2,1)}) %all-reduce.5.cloned.1.call-update) | async-done | bytes 1310736 | tf_op jit(solution)/shard_map/psum | solution.py:177
  241.6 7.0 %all-to-all-start.1 = ((bf16[16,40,1024]{2,1,0:T(8,128)(2,1)}), bf16[16,40,1024]{2,1,0:T(8,128)(2,1)S(1)}, u32[]{:S(2)}, u32[]{:S(2)}) async-start(bf16[16,40,1024]{2,1,0:T(8,128)(2,1)} %all-reduce.5.cloned.1.call-done), calls=%async_computation.1 | async-start | bytes 2621440 | tf_op jit(solution)/shard_map/all_to_all | solution.py:181
  248.6 0.6 gather_fusion.2
  249.3 0.3 select_reduce_fusion
  249.6 23.0 %all-to-all-done.1 = bf16[16,40,1024]{2,1,0:T(8,128)(2,1)S(1)} async-done(((bf16[16,40,1024]{2,1,0:T(8,128)(2,1)}), bf16[16,40,1024]{2,1,0:T(8,128)(2,1)S(1)}, u32[]{:S(2)}, u32[]{:S(2)}) %all-to-all-start.1) | async-done | bytes 1310752 | tf_op jit(solution)/shard_map/all_to_all | solution.py:181
  272.7 1.0 fusion.10
  273.7 0.3 fusion.28
  274.0 0.6 gather_fusion
  274.5 22.0 %all-gather.1 = bf16[16,4,1024]{2,1,0:T(4,128)(2,1)S(1)} all-gather(bf16[1,4,1024]{2,1,0:T(4,128)(2,1)S(1)} %bitcast.160), channel_id=2, replica_groups=mesh['req'=16,'tp'=8] {'req'}, dimensions={0}, use_global_device_ids=true | all-gather | bytes 139264 | tf_op jit(solution)/shard_map/all_gather | solution.py:210
  296.6 1.0 scatter_custom_fusion.2
  297.7 2.3 gather_fusion.4
  300.0 2.0 scatter_fusion
  (110 shorter events, 2.5 us)
Async XLA Ops:
  8.0 170.9 %copy-start = (bf16[1,352,1024]{2,1,0:T(8,128)(2,1)S(1)}, bf16[1,352,1024]{2,1,0:T(8,128)(2,1)}, u32[]{:S(2)}) copy-start(bf16[1,352,1024]{2,1,0:T(8,128)(2,1)} %param.38) | copy-start | bytes 2162692
  8.0 130.1 %all-reduce.3.cloned.1.call-start = ((), (), s32[]{:S(2)}) async-start(), calls=%async_computation.2 | async-start | bytes 2097152 | tf_op jit(solution)/shard_map/psum | solution.py:144
  14.4 8.4 %copy-start.24 = (s32[32]{0:T(128)}, s32[32]{0:T(128)S(1)}, u32[]{:S(2)}) copy-start(s32[32]{0:T(128)S(1)} %convert_reduce_fusion) | copy-start | bytes 388
  15.9 6.9 %copy-start.29 = (s32[32]{0:T(128)}, s32[32]{0:T(128)S(1)}, u32[]{:S(2)}) copy-start(s32[32]{0:T(128)S(1)} %pad_add_fusion) | copy-start | bytes 388
  15.9 7.1 %copy-start.3 = (bf16[256,1024]{1,0:T(8,128)(2,1)S(1)}, bf16[256,1024]{1,0:T(8,128)(2,1)}, u32[]{:S(2)}) copy-start(bf16[256,1024]{1,0:T(8,128)(2,1)} %param.20) | copy-start | bytes 1572868
  15.9 7.3 %copy-start.2 = (bf16[2,8,512,128]{3,2,1,0:T(8,128)(2,1)S(1)}, bf16[2,8,512,128]{3,2,1,0:T(8,128)(2,1)}, u32[]{:S(2)}) copy-start(bf16[2,8,512,128]{3,2,1,0:T(8,128)(2,1)} %param.21) | copy-start | bytes 6291460
  23.2 16.1 %copy-start.23 = (f32[256]{0:T(256)}, f32[256]{0:T(256)S(1)}, u32[]{:S(2)}) copy-start(f32[256]{0:T(256)S(1)} %add_rsqrt_fusion.1) | copy-start | bytes 3076
  32.3 7.0 %copy-start.26 = (bf16[1024,128]{1,0:T(8,128)(2,1)S(1)}, bf16[1024,128]{1,0:T(8,128)(2,1)}, u32[]{:S(2)}) copy-start(bf16[1024,128]{1,0:T(8,128)(2,1)} %param.29) | copy-start | bytes 786436
  32.3 7.0 %copy-start.28 = (f32[1024]{0:T(1024)S(1)}, f32[1024]{0:T(1024)}, u32[]{:S(2)}) copy-start(f32[1024]{0:T(1024)} %param.28) | copy-start | bytes 12292
  32.3 7.5 %copy-start.27 = (bf16[1024,128]{1,0:T(8,128)(2,1)S(1)}, bf16[1024,128]{1,0:T(8,128)(2,1)}, u32[]{:S(2)}) copy-start(bf16[1024,128]{1,0:T(8,128)(2,1)} %param.30) | copy-start | bytes 786436
  32.3 9.2 %copy-start.21 = (f32[32,2]{0,1:T(2,128)S(1)}, f32[32,2]{0,1:T(2,128)}, u32[]{:S(2)}) copy-start(f32[32,2]{0,1:T(2,128)} %param.27) | copy-start | bytes 772
  39.3 7.3 %copy-start.8 = (s32[256,64]{0,1:T(8,128)S(1)}, s32[256,64]{0,1:T(8,128)}, u32[]{:S(2)}) copy-start(s32[256,64]{0,1:T(8,128)} %subtract_clamp_fusion.1) | copy-start | bytes 196612
  39.3 7.3 %copy-start.16 = (pred[256,64]{0,1:T(8,128)(4,1)S(1)}, pred[256,64]{0,1:T(8,128)(4,1)}, u32[]{:S(2)}) copy-start(pred[256,64]{0,1:T(8,128)(4,1)} %get-tuple-element.21) | copy-start | bytes 49156
  39.3 7.3 %copy-start.22 = (f32[32,2]{0,1:T(2,128)S(1)}, f32[32,2]{0,1:T(2,128)}, u32[]{:S(2)}) copy-start(f32[32,2]{0,1:T(2,128)} %param.27) | copy-start | bytes 772
  39.3 7.3 %copy-start.25 = (s32[32]{0:T(128)S(1)}, s32[32]{0:T(128)}, u32[]{:S(2)}) copy-start(s32[32]{0:T(128)} %copy-done.24) | copy-start | bytes 388
  39.4 7.3 %copy-start.30 = (s32[32]{0:T(128)S(1)}, s32[32]{0:T(128)}, u32[]{:S(2)}) copy-start(s32[32]{0:T(128)} %copy-done.29) | copy-start | bytes 388
  40.8 6.8 %copy-start.4 = (bf16[1,8,512,128]{2,3,1,0:T(8,128)(2,1)S(1)}, bf16[1,8,512,128]{2,3,1,0:T(8,128)(2,1)}, u32[]{:S(2)}) copy-start(bf16[1,8,512,128]{2,3,1,0:T(8,128)(2,1)} %copy.113) | copy-start | bytes 3145732
  49.9 3.4 %copy-start.1 = (f32[2,256,8,512]{3,1,2,0:T(8,128)}, f32[2,256,8,512]{3,1,2,0:T(8,128)S(1)}, u32[]{:S(2)}) copy-start(f32[2,256,8,512]{3,1,2,0:T(8,128)S(1)} %get-tuple-element.26) | copy-start | bytes 25165828
  49.9 4.1 %copy-start.12 = (f32[2,256]{1,0:T(2,128)}, f32[2,256]{1,0:T(2,128)S(1)}, u32[]{:S(2)}) copy-start(f32[2,256]{1,0:T(2,128)S(1)} %maximum_maximum_fusion) | copy-start | bytes 6148
  54.1 0.6 copy-start.17
  65.8 3.2 %copy-start.5 = (bf16[1,8,512,128]{2,3,1,0:T(8,128)(2,1)S(1)}, bf16[1,8,512,128]{2,3,1,0:T(8,128)(2,1)}, u32[]{:S(2)}) copy-start(bf16[1,8,512,128]{2,3,1,0:T(8,128)(2,1)} %copy.115) | copy-start | bytes 3145732
  65.8 3.2 %copy-start.10 = (bf16[256,128]{0,1:T(8,128)(2,1)S(1)}, bf16[256,128]{0,1:T(8,128)(2,1)}, u32[]{:S(2)}) copy-start(bf16[256,128]{0,1:T(8,128)(2,1)} %convolution_convert_fusion.2) | copy-start | bytes 196612
  65.8 3.3 %copy-start.13 = (f32[2,256]{1,0:T(2,128)S(1)}, f32[2,256]{1,0:T(2,128)}, u32[]{:S(2)}) copy-start(f32[2,256]{1,0:T(2,128)} %copy-done.12) | copy-start | bytes 6148
  65.8 3.3 %copy-start.18 = (f32[2,256]{1,0:T(2,128)S(1)}, f32[2,256]{1,0:T(2,128)}, u32[]{:S(2)}) copy-start(f32[2,256]{1,0:T(2,128)} %copy-done.17) | copy-start | bytes 6148
  65.9 3.3 %copy-start.20 = (f32[256,2]{0,1:T(2,128)S(1)}, f32[256,2]{0,1:T(2,128)}, u32[]{:S(2)}) copy-start(f32[256,2]{0,1:T(2,128)} %get-tuple-element.10) | copy-start | bytes 6148
  69.1 5.2 %copy-start.7 = (bf16[128,1024]{1,0:T(8,128)(2,1)S(1)}, bf16[128,1024]{1,0:T(8,128)(2,1)}, u32[]{:S(2)}) copy-start(bf16[128,1024]{1,0:T(8,128)(2,1)} %param.32) | copy-start | bytes 786436
  69.1 6.5 %copy-start.15 = (s32[256,2]{0,1:T(2,128)S(1)}, s32[256,2]{0,1:T(2,128)}, u32[]{:S(2)}) copy-start(s32[256,2]{0,1:T(2,128)} %param.35) | copy-start | bytes 6148
  74.3 65.3 %copy-start.19 = (f32[1024]{0:T(1024)S(1)}, f32[1024]{0:T(1024)}, u32[]{:S(2)}) copy-start(f32[1024]{0:T(1024)} %param.33) | copy-start | bytes 12292
  140.4 11.6 %copy-start.9 = (s32[4096]{0:T(1024)S(1)}, s32[4096]{0:T(1024)}, u32[]{:S(2)}) copy-start(s32[4096]{0:T(1024)} %param.39) | copy-start | bytes 49156
  140.4 12.5 %copy-start.11 = (bf16[256,128]{0,1:T(8,128)(2,1)S(1)}, bf16[256,128]{0,1:T(8,128)(2,1)}, u32[]{:S(2)}) copy-start(bf16[256,128]{0,1:T(8,128)(2,1)} %convolution_convert_fusion.2) | copy-start | bytes 196612
  144.9 31.2 %all-to-all-start = ((bf16[16,40,1024]{2,1,0:T(8,128)(2,1)}), bf16[16,40,1024]{2,1,0:T(8,128)(2,1)S(1)}, u32[]{:S(2)}, u32[]{:S(2)}) async-start(bf16[16,40,1024]{2,1,0:T(8,128)(2,1)} %bitcast.149), calls=%async_computation | async-start | bytes 2621440 | tf_op jit(solution)/shard_map/all_to_all | solution.py:172
  151.9 89.7 %all-reduce.5.cloned.1.call-start = ((), (), s32[]{:S(2)}) async-start(), calls=%async_computation.3 | async-start | bytes 2621440 | tf_op jit(solution)/shard_map/psum | solution.py:177
  183.2 114.4 %all-gather.4.cloned.1.call-start = ((), (), s32[]{:S(2)}) async-start(), calls=%async_computation.4 | async-start | bytes 2228224 | tf_op jit(solution)/shard_map/all_gather | solution.py:211
  191.5 57.8 %copy-start.14 = (bf16[1024,16]{0,1:T(8,128)(2,1)S(1)}, bf16[1024,16]{0,1:T(8,128)(2,1)}, u32[]{:S(2)}) copy-start(bf16[1024,16]{0,1:T(8,128)(2,1)} %param.34) | copy-start | bytes 98308
  241.6 31.1 %all-to-all-start.1 = ((bf16[16,40,1024]{2,1,0:T(8,128)(2,1)}), bf16[16,40,1024]{2,1,0:T(8,128)(2,1)S(1)}, u32[]{:S(2)}, u32[]{:S(2)}) async-start(bf16[16,40,1024]{2,1,0:T(8,128)(2,1)} %all-reduce.5.cloned.1.call-done), calls=%async_computation.1 | async-start | bytes 2621440 | tf_op jit(solution)/shard_map/all_to_all | solution.py:181
  297.6 4.4 %copy-start.6 = (bf16[256,1024]{1,0:T(8,128)(2,1)}, bf16[256,1024]{1,0:T(8,128)(2,1)S(1)}, u32[]{:S(2)}) copy-start(bf16[256,1024]{1,0:T(8,128)(2,1)S(1)} %scatter_custom_fusion.2) | copy-start | bytes 1572868
Sparse Core Ops, SparseCore 0:
  75.7 62.3 all-reduce.2
  183.3 58.1 all-reduce.4
Sparse Core Ops, SparseCore 1:
  196.3 42.1 all-gather.3
where the time goes:
time: 311 us; the launch traced here: 309 us
  waiting for transfers between devices  133 us (43%)
  local copies, waits for them, and re-layouts  59.9 us (19%)
  other arithmetic  33 us (11%)
  matrix products  31.5 us (10%)
  blocking collectives  22 us (7%)
  between operations  16.2 us (5%)
  starting transfers between devices  14.1 us (5%)
    psum x1, waiting for transfers between devices, body(): attn = lax.psum(partial_attn, 'tp')  60.5 us
    psum x1, waiting for transfers between devices, body(): lax.psum(jnp.dot(act, down_mat, preferred_element_type=jnp.float32).astyp...  28.9 us
    all_to_all x1, waiting for transfers between devices, body(): lax.all_to_all(back, 'req', split_axis=0, concat_axis=0, tiled=True)  23 us
    all_gather x1, blocking collectives, body(): lax.all_gather(send_rows, 'req', axis=0, tiled=True)  22 us
    all_to_all x1, waiting for transfers between devices, body(): lax.all_to_all(outgoing, 'req', split_axis=0, concat_axis=0, tiled=True)  20.2 us
    unnamed x68, local copies, waits for them, and re-layouts  18.9 us
    scatter x1, local copies, waits for them, and re-layouts, body(): source_of = jnp.zeros((total_reqs,), jnp.int32).at[new_slot].set(everyone)  15.5 us
    select_n x1, other arithmetic, body(): tail_new = jnp.where(write_row[None, :, :, None], fresh, tail_kv)  8.26 us
  transfers between devices with their start and end apart: 5, of which 4 were waited for; matrix products, arithmetic and copies ran while one was open for 13% of the time, Pallas kernels for 0%

commit v1 on v0

--- a/solution.py
+++ b/solution.py
@@ -174,8 +174,11 @@
     gate_h = jnp.dot(flat, gate_mat, preferred_element_type=jnp.float32)
     up_h = jnp.dot(flat, up_mat, preferred_element_type=jnp.float32)
     act = (jax.nn.gelu(gate_h, approximate=True) * up_h).astype(jnp.bfloat16)
-    summed = lax.psum(
-        jnp.dot(act, down_mat, preferred_element_type=jnp.float32).astype(jnp.bfloat16), "tp"
+    summed = jnp.sum(
+        lax.all_gather(
+            jnp.dot(act, down_mat, preferred_element_type=jnp.float32).astype(jnp.bfloat16), "tp"
+        ),
+        axis=0,
     )
     back = summed.reshape(received.shape)
     result = lax.all_to_all(back, "req", split_axis=0, concat_axis=0, tiled=True)

time: 311 us -> 336 us (1.080)
  blocking collectives: 22 us -> 51.2 us
  other arithmetic: 33 us -> 41.1 us
  waiting for transfers between devices: 133 us -> 125 us
  starting transfers between devices: 14.1 us -> 7.34 us
    all_gather x1, waiting for transfers between devices: 0.03 us -> 44.5 us  [body(): lax.all_gather(send_tail, 'req', axis=0, tiled=True)]
    psum x1 -> x0, waiting for transfers between devices: 28.9 us -> none  [body(): lax.psum(jnp.dot(act, down_mat, preferred_element_type=jnp.float32).astyp...]
    all_to_all x0 -> x1, blocking collectives: none -> 28.2 us  [body(): lax.all_to_all(outgoing, 'req', split_axis=0, concat_axis=0, tiled=True)]
    all_to_all x1, waiting for transfers between devices: 23 us -> 0.01 us  [body(): lax.all_to_all(back, 'req', split_axis=0, concat_axis=0, tiled=True)]
    all_to_all x1 -> x0, waiting for transfers between devices: 20.2 us -> none  [body(): lax.all_to_all(outgoing, 'req', split_axis=0, concat_axis=0, tiled=True)]
    all_gather x0 -> x1, waiting for transfers between devices: none -> 19.9 us  [body(): lax.all_gather(jnp.dot(act, down_mat, preferred_element_type=jnp.float32)...]
    reduce_sum x0 -> x1, other arithmetic: none -> 8.08 us  [body(): jnp.sum(lax.all_gather(jnp.dot(act, down_mat, preferred_element_type=jnp....]
    all_to_all x1 -> x0, starting transfers between devices: 6.98 us -> none  [body(): lax.all_to_all(outgoing, 'req', split_axis=0, concat_axis=0, tiled=True)]
  transfers between devices with their start and end apart: 5 -> 4, of which waited for: 4 -> 3; matrix products, arithmetic and copies ran while one was open for 13% -> 15% of each run, Pallas kernels for 0% -> 0%
where the time goes in v1:
time: 336 us; the launch traced here: 335 us
  waiting for transfers between devices  125 us (37%)
  local copies, waits for them, and re-layouts  63.2 us (19%)
  blocking collectives  51.2 us (15%)
  other arithmetic  41.1 us (12%)
  matrix products  32.6 us (10%)
  between operations  14.3 us (4%)
  starting transfers between devices  7.34 us (2%)
    psum x1, waiting for transfers between devices, body(): attn = lax.psum(partial_attn, 'tp')  60.5 us
    all_gather x1, waiting for transfers between devices, body(): lax.all_gather(send_tail, 'req', axis=0, tiled=True)  44.5 us
    all_to_all x1, blocking collectives, body(): lax.all_to_all(outgoing, 'req', split_axis=0, concat_axis=0, tiled=True)  28.2 us
    all_gather x1, blocking collectives, body(): lax.all_gather(send_rows, 'req', axis=0, tiled=True)  23 us
    unnamed x48, local copies, waits for them, and re-layouts  22.3 us
    all_gather x1, waiting for transfers between devices, body(): lax.all_gather(jnp.dot(act, down_mat, preferred_element_type=jnp.float32)...  19.9 us
    scatter x1, local copies, waits for them, and re-layouts, body(): source_of = jnp.zeros((total_reqs,), jnp.int32).at[new_slot].set(everyone)  15.5 us
    dot_general x2, matrix products, bias_lookup(): jnp.einsum('rjk,kh->hrj', within.astype(jnp.float32), bias_table, precisi...  8.69 us
  transfers between devices with their start and end apart: 4, of which 3 were waited for; matrix products, arithmetic and copies ran while one was open for 15% of the time, Pallas kernels for 0%

profile of v1, /device:TPU:6, one launch (start us, length us, event | category | flops | bytes accessed | tf_op | source)
XLA Modules:
  0.0 334.7 jit_solution(240469363588978349)
XLA Ops:
  7.2 1.3 iota_compare_fusion.11
  8.5 0.8 select_reduce_fusion.2
  9.4 0.7 add.169
  10.1 1.3 iota_compare_fusion.5
  11.4 1.3 subtract_clamp_fusion.1
  12.7 0.8 convert_reduce_fusion
  13.5 1.2 slice.45
  15.1 6.9 %fusion.8 = f32[2,256,512]{2,0,1:T(2,128)S(1)} fusion(s32[256,512]{1,0:T(8,128)S(1)} %subtract_clamp_fusion, s32[32]{0:T(128)S(1)} %pad_add_fusion, s32[32]{0:T(128)S(1)} %convert_reduce_fusion, f32[32,2]{0,1:T(2,128)} %param.27), kind=kOutput, calls=%fused_computation.35 | convolution fusion | flops 113246208 | bytes 1573376 | tf_op jit(solution)/shard_map/rjk,kh->hrj/dot_general | solution.py:21
  22.0 0.2 copy.78
  22.4 1.2 fusion.90
  23.6 1.3 copy.113
  24.9 6.5 %fusion.89 = (bf16[1,256,64,128]{3,2,1,0:T(8,128)(2,1)}, bf16[1,256,64,128]{3,2,1,0:T(8,128)(2,1)}) fusion(bf16[2,256,64,128]{3,2,1,0:T(8,128)(2,1)} %param.22), kind=kLoop, calls=%fused_computation.187 | loop fusion | bytes 16777216 | tf_op jit(solution)/shard_map/slice | solution.py:59
  31.5 7.0 %copy.114 = bf16[1,256,64,128]{1,3,2,0:T(8,128)(2,1)} copy(bf16[1,256,64,128]{3,2,1,0:T(8,128)(2,1)} %get-tuple-element.12) | data formatting | bytes 8388608
  38.5 0.4 bitcast_convert_fusion.1
  38.9 1.1 convolution_convert_fusion.3
  40.0 0.6 iota_compare_fusion.12
  40.7 1.3 broadcast_and_fusion
  41.9 3.7 %multiply_reduce_fusion.1 = f32[2,256,64]{1,0,2:T(2,128)S(1)} fusion(bf16[2,256,64,64]{1,2,0,3:T(8,128)(2,1)} %bitcast.146, f32[2,256,64]{1,2,0:T(8,128)S(1)} %get-tuple-element.27), kind=kLoop, calls=%fused_computation.13 | loop fusion | flops 6258688 | bytes 4456448 | tf_op jit(solution)/shard_map/rhd,rthd->hrt/dot_general | solution.py:79
  45.6 1.8 fusion.92
  47.5 2.2 fusion.5
  49.8 3.3 copy-done.1
  53.1 2.6 fusion.4
  55.8 0.7 convert_bitcast_fusion
  56.6 0.5 copy-done.12
  57.0 6.9 %copy.116 = bf16[1,256,64,128]{1,3,2,0:T(8,128)(2,1)} copy(bf16[1,256,64,128]{3,2,1,0:T(8,128)(2,1)} %get-tuple-element.13) | data formatting | bytes 8388608
  64.0 2.0 convolution_convert_fusion.2
  66.0 2.3 copy.115
  68.2 3.1 multiply_reduce_fusion
  71.4 6.3 %fusion.19 = bf16[256,2,64]{0,2,1:T(8,128)(2,1)S(1)} fusion(f32[256,2,64]{0,2,1:T(8,128)S(1)} %multiply_reduce_fusion, f32[2,256,8,512]{3,1,2,0:T(8,128)} %copy-done.1, f32[2,256]{1,0:T(2,128)} %copy-done.12, f32[2,256]{1,0:T(2,128)} %copy-done.9, f32[2,256,512]{2,1,0:T(8,128)S(1)} %copy.78, pred[256,8,512]{2,0,1:T(8,128)(4,1)S(1)} %broadcast_and_fusion, ...), kind=kOutput, calls=%fused_computation.52 | convolution fusion | flops 281182208 | bytes 11802624 | tf_op jit(solution)/shard_map/hrgj,gjhd->rhd/dot_general | solution.py:93
  77.7 1.3 fusion.93
  79.5 1.2 reduce-window.14
  80.7 0.2 slice_reduce_fusion
  81.1 60.5 %all-reduce.2.cloned.1.call-done = f32[256,1024]{1,0:T(8,128)} async-done(((f32[256,1024]{1,0:T(8,128)}), f32[256,1024]{1,0:T(8,128)}) %all-reduce.2.cloned.1.call-update) | async-done | bytes 1048592 | tf_op jit(solution)/shard_map/psum | solution.py:144
  141.6 1.5 fusion.24
  143.0 0.2 fusion.26
  143.2 0.5 broadcast_in_dim.97
  143.8 1.2 reshape.353
  145.0 2.2 convolution_convert_fusion.1
  147.2 28.2 %all_to_all.10 = bf16[16,40,1024]{2,1,0:T(8,128)(2,1)S(1)} all-to-all(bf16[16,40,1024]{2,1,0:T(8,128)(2,1)S(1)} %bitcast.150), channel_id=1, replica_groups=mesh['req'=16,'tp'=8] {'req'}, dimensions={0} | all-to-all | bytes 2621440 | tf_op jit(solution)/shard_map/all_to_all | solution.py:172
  175.4 2.8 fusion.48
  178.2 4.4 %convolution_convert_fusion = bf16[640,1024]{1,0:T(8,128)(2,1)} fusion(bf16[640,1024]{1,0:T(8,128)(2,1)S(1)} %bitcast.152, f32[640,352]{0,1:T(8,128)} %fusion.48, bf16[1,352,1024]{2,1,0:T(8,128)(2,1)S(1)} %copy-done, bf16[1,1024,352]{1,2,0:T(8,128)(2,1)} %param.37), kind=kOutput, calls=%fused_computation.27 | convolution fusion | flops 925655040 | bytes 4964352 | tf_op jit(solution)/shard_map/dot_general | solution.py:179
  182.7 0.8 reduce-window.16
  183.5 0.2 slice_reduce_fusion.1
  184.2 0.7 convert_reduce_fusion.1
  184.9 1.4 scatter_custom_fusion
  186.3 0.7 compare_select_fusion.2
  186.9 8.4 %broadcast_select_fusion = bf16[2,256,64,128]{3,2,1,0:T(8,128)(2,1)} fusion(bf16[2,256,64,128]{3,2,1,0:T(8,128)(2,1)} %param.22, pred[256,64]{1,0:T(8,128)(4,1)S(1)} %copy.89, bf16[2,256,128]{2,1,0:T(8,128)(2,1)S(1)} %copy.90), kind=kLoop, calls=%fused_computation.20 | loop fusion | flops 4194304 | bytes 16924672 | tf_op jit(solution)/shard_map/jit(_where)/select_n | solution.py:142
  195.3 4.8 %gather_fusion.3 = bf16[4,2,64,128]{3,2,1,0:T(8,128)(2,1)} fusion(bf16[2,256,64,128]{3,2,1,0:T(8,128)(2,1)} %broadcast_select_fusion, s32[1024]{0:T(1024)S(1)} %pad_clamp_fusion.3), kind=kCustom, calls=%fused_computation.4 | custom fusion | bytes 262160 | tf_op jit(solution)/shard_map/gather | solution.py:211
  200.4 15.5 %scatter_custom_fusion.1 = s32[4096]{0:T(1024)S(1)} fusion(s32[4096]{0:T(1024)S(1)} %add_select_fusion.1, s32[4096]{0:T(1024)S(1)} %iota.80, s32[]{:T(128)} %constant.37.clone.1), kind=kCustom, calls=%fused_computation.136 | custom fusion | bytes 16388 | tf_op jit(solution)/shard_map/scatter | solution.py:201
  215.9 0.6 gather_fusion.1
  216.5 19.9 %all-gather.8.cloned.1.call-done = bf16[5120,1024]{1,0:T(8,128)(2,1)} async-done(((bf16[640,1024]{1,0:T(8,128)(2,1)}), bf16[5120,1024]{1,0:T(8,128)(2,1)}) %all-gather.8.cloned.1.call-update) | async-done | bytes 10485776 | tf_op jit(solution)/shard_map/all_gather | solution.py:178
  236.4 8.1 %reduce_sum.124 = bf16[640,1024]{1,0:T(8,128)(2,1)} reduce(bf16[8,640,1024]{2,1,0:T(8,128)(2,1)} %bitcast.148, bf16[]{:T(256)} %constant.90.clone.1), dimensions={0}, to_apply=%region_15.16 | reduce | flops 4587520 | bytes 11796482 | tf_op jit(solution)/shard_map/reduce_sum | solution.py:177
  244.5 7.2 %all-to-all-start.1 = ((bf16[16,40,1024]{2,1,0:T(8,128)(2,1)}), bf16[16,40,1024]{2,1,0:T(8,128)(2,1)S(1)}, u32[]{:S(2)}, u32[]{:S(2)}) async-start(bf16[16,40,1024]{2,1,0:T(8,128)(2,1)} %bitcast.39), calls=%async_computation.1 | async-start | bytes 2621440 | tf_op jit(solution)/shard_map/all_to_all | solution.py:184
  251.8 0.6 gather_fusion.2
  252.5 0.3 select_reduce_fusion
  252.8 44.5 %all-gather.6.cloned.1.call-done = bf16[64,2,64,128]{3,2,1,0:T(8,128)(2,1)} async-done(((bf16[4,2,64,128]{3,2,1,0:T(8,128)(2,1)}), bf16[64,2,64,128]{3,2,1,0:T(8,128)(2,1)}) %all-gather.6.cloned.1.call-update) | async-done | bytes 2097168 | tf_op jit(solution)/shard_map/all_gather | solution.py:214
  297.2 2.2 gather_fusion.4
  299.4 2.0 scatter_fusion
  301.4 1.0 fusion.10
  302.5 0.3 fusion.28
  302.7 0.6 gather_fusion
  303.3 23.0 %all-gather.2 = bf16[16,4,1024]{2,1,0:T(4,128)(2,1)S(1)} all-gather(bf16[1,4,1024]{2,1,0:T(4,128)(2,1)S(1)} %bitcast.161), channel_id=3, replica_groups=mesh['req'=16,'tp'=8] {'req'}, dimensions={0}, use_global_device_ids=true | all-gather | bytes 139264 | tf_op jit(solution)/shard_map/all_gather | solution.py:213
  326.3 1.0 scatter_custom_fusion.2
  327.4 0.8 copy-done.5
  (90 shorter events, 2.6 us)
Async XLA Ops:
  7.2 171.1 %copy-start = (bf16[1,352,1024]{2,1,0:T(8,128)(2,1)S(1)}, bf16[1,352,1024]{2,1,0:T(8,128)(2,1)}, u32[]{:S(2)}) copy-start(bf16[1,352,1024]{2,1,0:T(8,128)(2,1)} %param.38) | copy-start | bytes 2162692
  7.2 134.4 %all-reduce.2.cloned.1.call-start = ((), (), s32[]{:S(2)}) async-start(), calls=%async_computation.2 | async-start | bytes 2097152 | tf_op jit(solution)/shard_map/psum | solution.py:144
  13.5 8.4 %copy-start.16 = (s32[32]{0:T(128)}, s32[32]{0:T(128)S(1)}, u32[]{:S(2)}) copy-start(s32[32]{0:T(128)S(1)} %convert_reduce_fusion) | copy-start | bytes 388
  15.0 6.9 %copy-start.20 = (s32[32]{0:T(128)}, s32[32]{0:T(128)S(1)}, u32[]{:S(2)}) copy-start(s32[32]{0:T(128)S(1)} %pad_add_fusion) | copy-start | bytes 388
  15.1 7.1 %copy-start.3 = (bf16[256,1024]{1,0:T(8,128)(2,1)S(1)}, bf16[256,1024]{1,0:T(8,128)(2,1)}, u32[]{:S(2)}) copy-start(bf16[256,1024]{1,0:T(8,128)(2,1)} %param.20) | copy-start | bytes 1572868
  15.1 7.3 %copy-start.2 = (bf16[2,8,512,128]{3,2,1,0:T(8,128)(2,1)S(1)}, bf16[2,8,512,128]{3,2,1,0:T(8,128)(2,1)}, u32[]{:S(2)}) copy-start(bf16[2,8,512,128]{3,2,1,0:T(8,128)(2,1)} %param.21) | copy-start | bytes 6291460
  22.4 16.1 %copy-start.15 = (f32[256]{0:T(256)}, f32[256]{0:T(256)S(1)}, u32[]{:S(2)}) copy-start(f32[256]{0:T(256)S(1)} %add_rsqrt_fusion.1) | copy-start | bytes 3076
  31.5 7.0 %copy-start.17 = (bf16[1024,128]{1,0:T(8,128)(2,1)S(1)}, bf16[1024,128]{1,0:T(8,128)(2,1)}, u32[]{:S(2)}) copy-start(bf16[1024,128]{1,0:T(8,128)(2,1)} %param.29) | copy-start | bytes 786436
  31.5 7.0 %copy-start.19 = (f32[1024]{0:T(1024)S(1)}, f32[1024]{0:T(1024)}, u32[]{:S(2)}) copy-start(f32[1024]{0:T(1024)} %param.28) | copy-start | bytes 12292
  31.5 7.4 %copy-start.18 = (bf16[1024,128]{1,0:T(8,128)(2,1)S(1)}, bf16[1024,128]{1,0:T(8,128)(2,1)}, u32[]{:S(2)}) copy-start(bf16[1024,128]{1,0:T(8,128)(2,1)} %param.30) | copy-start | bytes 786436
  31.5 9.1 %copy-start.14 = (f32[32,2]{0,1:T(2,128)S(1)}, f32[32,2]{0,1:T(2,128)}, u32[]{:S(2)}) copy-start(f32[32,2]{0,1:T(2,128)} %param.27) | copy-start | bytes 772
  38.5 9.0 %copy-start.4 = (bf16[1,8,512,128]{2,3,1,0:T(8,128)(2,1)S(1)}, bf16[1,8,512,128]{2,3,1,0:T(8,128)(2,1)}, u32[]{:S(2)}) copy-start(bf16[1,8,512,128]{2,3,1,0:T(8,128)(2,1)} %copy.113) | copy-start | bytes 3145732
  49.7 3.4 %copy-start.1 = (f32[2,256,8,512]{3,1,2,0:T(8,128)}, f32[2,256,8,512]{3,1,2,0:T(8,128)S(1)}, u32[]{:S(2)}) copy-start(f32[2,256,8,512]{3,1,2,0:T(8,128)S(1)} %get-tuple-element.26) | copy-start | bytes 25165828
  49.8 6.8 %copy-start.9 = (f32[2,256]{1,0:T(2,128)}, f32[2,256]{1,0:T(2,128)S(1)}, u32[]{:S(2)}) copy-start(f32[2,256]{1,0:T(2,128)S(1)} %maximum_maximum_fusion) | copy-start | bytes 6148
  56.5 0.6 copy-start.12
  71.4 6.3 %copy-start.6 = (bf16[128,1024]{1,0:T(8,128)(2,1)S(1)}, bf16[128,1024]{1,0:T(8,128)(2,1)}, u32[]{:S(2)}) copy-start(bf16[128,1024]{1,0:T(8,128)(2,1)} %param.32) | copy-start | bytes 786436
  71.4 7.7 %copy-start.11 = (s32[256,2]{0,1:T(2,128)S(1)}, s32[256,2]{0,1:T(2,128)}, u32[]{:S(2)}) copy-start(s32[256,2]{0,1:T(2,128)} %param.35) | copy-start | bytes 6148
  71.4 71.7 %copy-start.13 = (f32[1024]{0:T(1024)S(1)}, f32[1024]{0:T(1024)}, u32[]{:S(2)}) copy-start(f32[1024]{0:T(1024)} %param.33) | copy-start | bytes 12292
  79.0 157.4 %all-gather.8.cloned.1.call-start = ((), (), s32[]{:S(2)}) async-start(), calls=%async_computation.4 | async-start | bytes 11796480 | tf_op jit(solution)/shard_map/all_gather | solution.py:178
  145.0 37.7 %copy-start.7 = (s32[4096]{0:T(1024)S(1)}, s32[4096]{0:T(1024)}, u32[]{:S(2)}) copy-start(s32[4096]{0:T(1024)} %param.39) | copy-start | bytes 49156
  145.0 38.9 %copy-start.8 = (bf16[256,128]{0,1:T(8,128)(2,1)S(1)}, bf16[256,128]{0,1:T(8,128)(2,1)}, u32[]{:S(2)}) copy-start(bf16[256,128]{0,1:T(8,128)(2,1)} %convolution_convert_fusion.2) | copy-start | bytes 196612
  182.6 114.6 %all-gather.6.cloned.1.call-start = ((), (), s32[]{:S(2)}) async-start(), calls=%async_computation.3 | async-start | bytes 2228224 | tf_op jit(solution)/shard_map/all_gather | solution.py:214
  195.3 57.2 %copy-start.10 = (bf16[1024,16]{0,1:T(8,128)(2,1)S(1)}, bf16[1024,16]{0,1:T(8,128)(2,1)}, u32[]{:S(2)}) copy-start(bf16[1024,16]{0,1:T(8,128)(2,1)} %param.34) | copy-start | bytes 98308
  244.5 56.9 %all-to-all-start.1 = ((bf16[16,40,1024]{2,1,0:T(8,128)(2,1)}), bf16[16,40,1024]{2,1,0:T(8,128)(2,1)S(1)}, u32[]{:S(2)}, u32[]{:S(2)}) async-start(bf16[16,40,1024]{2,1,0:T(8,128)(2,1)} %bitcast.39), calls=%async_computation.1 | async-start | bytes 2621440 | tf_op jit(solution)/shard_map/all_to_all | solution.py:184
  327.4 0.8 copy-start.5
Sparse Core Ops, SparseCore 0:
  79.1 62.3 all-reduce.1
  182.8 53.6 all-gather.7
  239.2 58.0 all-gather.5
